TPU v7x, 32 devices: a whole 2x2x4 slice. The times are simulated.
32 devices in a mesh: section: 2 (over x), fsdp: 16 (over z, y, core).
Axes of the slice: x: 2, y: 2, z: 4, core: 2. Of those that a mesh axis runs over, the one named last changes fastest.
Arguments:
- hidden_in: bfloat16 [16, 128, 4096], P('fsdp', 'section'), may hold values from -40 to 40
- queries: bfloat16 [2, 16, 128, 4096], P('section', 'fsdp'), may hold values from -260 to 260
- key_weight: bfloat16 [2, 4096, 512], P('section', 'fsdp'), may hold values from -0.09375 to 0.09375
- value_weight: bfloat16 [2, 4096, 512], P('section', 'fsdp'), may hold values from -0.09375 to 0.09375
- norm_gain: float32 [2, 4096], P('section'), may hold values from 0.5 to 1.5
Outputs:
- section_outputs: bfloat16 [2, 16, 128, 4096], P('section', 'fsdp')
All inputs are finite; a program needn't handle non-finite values.
Results may differ from a plain program's by a relative error of at most 0.013.
Values may be sent and summed in bfloat16 or wider, within the bound.
A program may use at most 64 MiB of HBM per device.

v0:
```python
import math

import jax
import jax.numpy as jnp
from jax import lax
from jax.sharding import PartitionSpec as P

QH = 32
KVH = 4
HD = 128


epsilon = 1e-05


def from_behind(value, axis, by):
    count = lax.axis_size(axis)
    pairs = [(i, i + by) for i in range(count) if 0 <= i + by < count]
    return lax.ppermute(value, axis, pairs)


def rms_norm(hidden, section_gain):
    hidden_f32 = hidden.astype(jnp.float32)
    mean_square = jnp.mean(hidden_f32 * hidden_f32, axis=-1, keepdims=True)
    return (hidden_f32 * lax.rsqrt(mean_square + epsilon) * section_gain).astype(jnp.bfloat16)


def rotate(heads, positions):
    half_width = heads.shape[-1] // 2
    frequency = jnp.exp(
        jnp.arange(half_width, dtype=jnp.float32) * (-2.0 * math.log(10000.0) / heads.shape[-1])
    )
    angles = positions[:, None] * frequency[None, :]
    cosine = jnp.cos(angles)[:, None, :]
    sine_table = jnp.sin(angles)[:, None, :]
    first_half = heads[..., :half_width]
    second_half = heads[..., half_width:]
    return jnp.concatenate(
        [
            first_half * cosine - second_half * sine_table,
            second_half * cosine + first_half * sine_table,
        ],
        axis=-1,
    )


def attend(query_heads, key_heads, value_heads, query_pos, key_pos):
    scores = jnp.einsum(
        "lkgd,rkd->kglr", query_heads, key_heads, preferred_element_type=jnp.float32
    )
    scores = scores * (1.0 / math.sqrt(HD))
    allowed = key_pos[None, :] <= query_pos[:, None]
    scores = jnp.where(allowed, scores, -1e30)
    row_max = jnp.max(scores, axis=-1, keepdims=True)
    weights = jnp.exp(scores - row_max)
    softmax_probs = (weights / jnp.sum(weights, axis=-1, keepdims=True)).astype(jnp.bfloat16)
    attn_mixed = jnp.einsum(
        "kglr,rkd->lkgd", softmax_probs, value_heads, preferred_element_type=jnp.float32
    )
    return attn_mixed.reshape(query_heads.shape[0], -1)


def body(hidden_in, queries, key_weight, value_weight, norm_gain):
    section_index = lax.axis_index("section")
    section_count = lax.axis_size("section")
    whole_in = lax.all_gather(hidden_in, "section", axis=1, tiled=True)[0]
    seq_rows = whole_in.shape[0]
    model_width = whole_in.shape[1]
    block_count = 4
    block_rows = seq_rows // block_count
    query_all = queries[0, 0]
    section_gain = norm_gain[0]
    kv_width = key_weight.shape[2]
    key_full, value_full = (
        lax.all_gather(key_weight[0], "fsdp", axis=0, tiled=True),
        lax.all_gather(value_weight[0], "fsdp", axis=0, tiled=True),
    )
    key_positions = jnp.arange(seq_rows, dtype=jnp.float32)

    def advance(moment, carry_state):
        arriving, key_cache, value_cache, outputs = carry_state
        block_index = moment - section_index
        active = (block_index >= 0) & (block_index < block_count)
        row_start = jnp.clip(block_index, 0, block_count - 1) * block_rows
        fresh_rows = lax.dynamic_slice_in_dim(whole_in, row_start, block_rows, 0)
        span_rows = jnp.where(section_index == 0, fresh_rows, arriving)

        def process(operands):
            span_rows, key_cache, value_cache, outputs = operands
            positions = row_start.astype(jnp.float32) + jnp.arange(block_rows, dtype=jnp.float32)
            normed = rms_norm(span_rows, section_gain)
            key_new = jnp.dot(normed, key_full, preferred_element_type=jnp.float32)
            value_new = jnp.dot(normed, value_full, preferred_element_type=jnp.float32)
            key_new = (
                rotate(key_new.reshape(block_rows, KVH, HD), positions)
                .astype(jnp.bfloat16)
                .reshape(block_rows, kv_width)
            )
            value_new = value_new.astype(jnp.bfloat16)
            key_cache = lax.dynamic_update_slice_in_dim(key_cache, key_new, row_start, 0)
            value_cache = lax.dynamic_update_slice_in_dim(value_cache, value_new, row_start, 0)
            query_rows = lax.dynamic_slice_in_dim(query_all, row_start, block_rows, 0)
            query_heads = rotate(
                query_rows.astype(jnp.float32).reshape(block_rows, QH, HD), positions
            ).astype(jnp.bfloat16)
            query_heads = query_heads.reshape(block_rows, KVH, QH // KVH, HD)
            attn_mixed = attend(
                query_heads,
                key_cache.reshape(seq_rows, KVH, HD),
                value_cache.reshape(seq_rows, KVH, HD),
                positions,
                key_positions,
            )
            result = (span_rows.astype(jnp.float32) + attn_mixed).astype(jnp.bfloat16)
            outputs = lax.dynamic_update_slice_in_dim(outputs, result, row_start, 0)
            return (result, key_cache, value_cache, outputs)

        def skipped(operands):
            return operands

        result, key_cache, value_cache, outputs = lax.cond(
            active, process, skipped, (span_rows, key_cache, value_cache, outputs)
        )
        arriving = from_behind(result, "section", 1)
        return (arriving, key_cache, value_cache, outputs)

    carry_state = (
        jnp.zeros((block_rows, model_width), jnp.bfloat16),
        jnp.zeros((seq_rows, kv_width), jnp.bfloat16),
        jnp.zeros((seq_rows, kv_width), jnp.bfloat16),
        jnp.zeros((seq_rows, model_width), jnp.bfloat16),
    )
    carry_state = advance(0, carry_state)

    def loop_step(moment, loop_state):
        return advance(moment, loop_state)

    carry_state = lax.fori_loop(1, block_count + section_count - 1, loop_step, carry_state)
    return carry_state[3][None, None]


def solution(mesh):
    placed = (
        P("fsdp", "section", None),
        P("section", "fsdp", None, None),
        P("section", "fsdp", None),
        P("section", "fsdp", None),
        P("section", None),
    )
    return jax.shard_map(
        body,
        mesh=mesh,
        in_specs=placed,
        out_specs=P("section", "fsdp", None, None),
        check_vma=False,
    )
```

profile of v0, /device:TPU:0, one launch (start us, length us, event | category | flops | bytes accessed | tf_op | source)
XLA Modules:
  0.0 290.1 jit_solution(10249490760738924448)
XLA Ops:
  8.8 24.2 %all-gather.6.cloned.1.call-done = bf16[1,128,4096]{2,1,0:T(8,128)(2,1)} async-done(((bf16[1,64,4096]{2,1,0:T(8,128)(2,1)}), bf16[1,128,4096]{2,1,0:T(8,128)(2,1)}) %all-gather.6.cloned.1.call-update) | async-done | bytes 1048592 | tf_op jit(solution)/shard_map/all_gather | solution.py:66
  33.9 51.6 %all-gather.8.cloned.1.call-done = bf16[1,4096,512]{2,1,0:T(8,128)(2,1)} async-done(((bf16[1,256,512]{2,1,0:T(8,128)(2,1)}), bf16[1,4096,512]{2,1,0:T(8,128)(2,1)}) %all-gather.8.cloned.1.call-update) | async-done | bytes 4194320 | tf_op jit(solution)/shard_map/all_gather | solution.py:76
  85.5 51.1 %all-gather.10.cloned.1.call-done = bf16[1,4096,512]{2,1,0:T(8,128)(2,1)} async-done(((bf16[1,256,512]{2,1,0:T(8,128)(2,1)}), bf16[1,4096,512]{2,1,0:T(8,128)(2,1)}) %all-gather.10.cloned.1.call-update) | async-done | bytes 4194320 | tf_op jit(solution)/shard_map/all_gather | solution.py:75
  136.6 22.1 %conditional.2 = (bf16[32,4096]{1,0:T(8,128)(2,1)S(1)}, bf16[128,512]{1,0:T(8,128)(2,1)}, bf16[128,512]{1,0:T(8,128)(2,1)}, bf16[128,4096]{1,0:T(8,128)(2,1)}) conditional(s32[]{:T(128)} %convert_element_type.65, bf16[32,4096]{1,0:T(8,128)(2,1)S(1)} %select_bitcast_fusion, (bf16[32,4096]{1,0:T(8,128)(2,1)S(1)}, f32[1,4096]{1,0:T(1,128)}, ...), branch_computations={%region_0.1_spmd, %region_1.5_spmd} | conditional | flops 373972352 | bytes 20551808 | solution.py:121
  136.6 1.0 convert_bitcast_fusion
  139.0 3.1 %fusion.17 = f32[32,512]{1,0:T(8,128)S(1)} fusion(bf16[4096,512]{1,0:T(8,128)(2,1)} %get-tuple-element.299, bf16[32,4096]{1,0:T(8,128)(2,1)S(1)} %get-tuple-element.294, f32[4096]{0:T(1024)S(1)} %bitcast.81, f32[32]{0:T(128)S(1)} %add_rsqrt_fusion), kind=kOutput, calls=%fused_computation.26 | convolution fusion | flops 134742016 | bytes 4538496 | tf_op jit(solution)/shard_map/cond/branch_1_fun/dot_general | solution.py:92
  143.0 1.4 dynamic_update_slice.13
  145.9 3.1 %convolution_convert_fusion = bf16[32,512]{1,0:T(8,128)(2,1)S(1)} fusion(bf16[4096,512]{1,0:T(8,128)(2,1)} %get-tuple-element.296, bf16[32,4096]{1,0:T(8,128)(2,1)S(1)} %get-tuple-element.294, f32[4096]{0:T(1024)S(1)} %bitcast.82, f32[32]{0:T(128)S(1)} %add_rsqrt_fusion), kind=kOutput, calls=%fused_computation.8 | convolution fusion | flops 134758400 | bytes 4505728 | tf_op jit(solution)/shard_map/cond/branch_1_fun/dot_general | solution.py:93
  149.7 1.4 dynamic_update_slice.12
  152.3 1.9 convolution_bitcast_fusion
  154.9 1.1 broadcast_in_dim.16
  155.9 2.8 dynamic_update_slice.14
  158.7 1.3 collective-permute-start.1
  160.0 6.2 %collective-permute-done.1 = bf16[32,4096]{1,0:T(8,128)(2,1)S(1)} collective-permute-done((bf16[32,4096]{1,0:T(8,128)(2,1)S(1)}, bf16[32,4096]{1,0:T(8,128)(2,1)S(1)}, u32[]{:S(2)}, u32[]{:S(2)}) %collective-permute-start.1) | collective-permute-done | bytes 262176 | tf_op jit(solution)/shard_map/ppermute | solution.py:19
  166.2 117.3 %while.21 = (s32[]{:T(128)}, bf16[32,4096]{1,0:T(8,128)(2,1)S(1)}, bf16[128,512]{1,0:T(8,128)(2,1)}, bf16[128,512]{1,0:T(8,128)(2,1)}, bf16[128,4096]{1,0:T(8,12...) while((s32[]{:T(128)}, bf16[32,4096]{1,0:T(8,128)(2,1)S(1)}, ...), condition=%wide.region_11.12_spmd.clone, body=%wide.region_5.11_spmd.clone.sunk | while | flops 374103424 | bytes 21077040 | solution.py:138
  167.2 19.8 %conditional.5 = ((bf16[32,4096]{1,0:T(8,128)(2,1)S(1)}, bf16[128,512]{1,0:T(8,128)(2,1)}, bf16[128,512]{1,0:T(8,128)(2,1)}, bf16[128,4096]{1,0:T(8,128)(2,1)})) conditional(s32[]{:T(128)} %convert_element_type.108, (bf16[32,4096]{1,0:T(8,128)(2,1)S(1)}, bf16[128,512]{1,0:T(8,128)(2,1)}, bf16[128,512]{1,0:T(8,128)(2,1)}, ...), branch_computations={%region_6.6_spmd, %region_7.10_spmd} | conditional | flops 373972352 | bytes 19241090 | solution.py:121
  167.3 1.0 convert_bitcast_fusion.1
  169.7 3.1 %fusion.45 = f32[32,512]{1,0:T(8,128)S(1)} fusion(bf16[4096,512]{1,0:T(8,128)(2,1)} %get-tuple-element.308, bf16[32,4096]{1,0:T(8,128)(2,1)S(1)} %get-tuple-element.301, f32[4096]{0:T(1024)S(1)} %bitcast.83, f32[32]{0:T(128)S(1)} %add_rsqrt_fusion.1), kind=kOutput, calls=%fused_computation.67 | convolution fusion | flops 134742016 | bytes 4538496 | tf_op jit(solution)/shard_map/while/body/eval_jaxpr/cond/branch_1_fun/dot_general | solution.py:92
  173.0 1.4 dynamic_update_slice.16
  176.0 3.1 %convolution_convert_fusion.1 = bf16[32,512]{1,0:T(8,128)(2,1)S(1)} fusion(bf16[4096,512]{1,0:T(8,128)(2,1)} %get-tuple-element.304, bf16[32,4096]{1,0:T(8,128)(2,1)S(1)} %get-tuple-element.301, f32[4096]{0:T(1024)S(1)} %bitcast.84, f32[32]{0:T(128)S(1)} %add_rsqrt_fusion.1), kind=kOutput, calls=%fused_computation.49 | convolution fusion | flops 134758400 | bytes 4505728 | tf_op jit(solution)/shard_map/while/body/eval_jaxpr/cond/branch_1_fun/dot_general | solution.py:93
  179.0 1.4 dynamic_update_slice.15
  181.7 1.9 convolution_bitcast_fusion.1
  184.2 2.8 dynamic_update_slice.17
  187.0 4.4 %collective-permute-start = (bf16[32,4096]{1,0:T(8,128)(2,1)S(1)}, bf16[32,4096]{1,0:T(8,128)(2,1)S(1)}, u32[]{:S(2)}, u32[]{:S(2)}) collective-permute-start(bf16[32,4096]{1,0:T(8,128)(2,1)S(1)} %get-tuple-element.486), channel_id=1, source_target_pairs={{0,16},{1,17},{2,18},{3,19},{4,20},{5,21},{6,22},{7,23},{8,24},{9,... | collective-permute-start | bytes 786440 | tf_op jit(solution)/shard_map/while/body/eval_jaxpr/ppermute | solution.py:19
  191.4 5.4 %collective-permute-done = bf16[32,4096]{1,0:T(8,128)(2,1)S(1)} collective-permute-done((bf16[32,4096]{1,0:T(8,128)(2,1)S(1)}, bf16[32,4096]{1,0:T(8,128)(2,1)S(1)}, u32[]{:S(2)}, u32[]{:S(2)}) %collective-permute-start) | collective-permute-done | bytes 262176 | tf_op jit(solution)/shard_map/while/body/eval_jaxpr/ppermute | solution.py:19
  197.8 19.8 %conditional.5 = ((bf16[32,4096]{1,0:T(8,128)(2,1)S(1)}, bf16[128,512]{1,0:T(8,128)(2,1)}, bf16[128,512]{1,0:T(8,128)(2,1)}, bf16[128,4096]{1,0:T(8,128)(2,1)})) conditional(s32[]{:T(128)} %convert_element_type.108, (bf16[32,4096]{1,0:T(8,128)(2,1)S(1)}, bf16[128,512]{1,0:T(8,128)(2,1)}, bf16[128,512]{1,0:T(8,128)(2,1)}, ...), branch_computations={%region_6.6_spmd, %region_7.10_spmd} | conditional | flops 373972352 | bytes 19241090 | solution.py:121
  197.8 1.0 convert_bitcast_fusion.1
  200.2 3.1 %fusion.45 = f32[32,512]{1,0:T(8,128)S(1)} fusion(bf16[4096,512]{1,0:T(8,128)(2,1)} %get-tuple-element.308, bf16[32,4096]{1,0:T(8,128)(2,1)S(1)} %get-tuple-element.301, f32[4096]{0:T(1024)S(1)} %bitcast.83, f32[32]{0:T(128)S(1)} %add_rsqrt_fusion.1), kind=kOutput, calls=%fused_computation.67 | convolution fusion | flops 134742016 | bytes 4538496 | tf_op jit(solution)/shard_map/while/body/eval_jaxpr/cond/branch_1_fun/dot_general | solution.py:92
  203.6 1.4 dynamic_update_slice.16
  206.5 3.1 %convolution_convert_fusion.1 = bf16[32,512]{1,0:T(8,128)(2,1)S(1)} fusion(bf16[4096,512]{1,0:T(8,128)(2,1)} %get-tuple-element.304, bf16[32,4096]{1,0:T(8,128)(2,1)S(1)} %get-tuple-element.301, f32[4096]{0:T(1024)S(1)} %bitcast.84, f32[32]{0:T(128)S(1)} %add_rsqrt_fusion.1), kind=kOutput, calls=%fused_computation.49 | convolution fusion | flops 134758400 | bytes 4505728 | tf_op jit(solution)/shard_map/while/body/eval_jaxpr/cond/branch_1_fun/dot_general | solution.py:93
  209.6 1.5 dynamic_update_slice.15
  212.3 1.9 convolution_bitcast_fusion.1
  214.8 2.8 dynamic_update_slice.17
  217.6 4.4 %collective-permute-start = (bf16[32,4096]{1,0:T(8,128)(2,1)S(1)}, bf16[32,4096]{1,0:T(8,128)(2,1)S(1)}, u32[]{:S(2)}, u32[]{:S(2)}) collective-permute-start(bf16[32,4096]{1,0:T(8,128)(2,1)S(1)} %get-tuple-element.486), channel_id=1, source_target_pairs={{0,16},{1,17},{2,18},{3,19},{4,20},{5,21},{6,22},{7,23},{8,24},{9,... | collective-permute-start | bytes 786440 | tf_op jit(solution)/shard_map/while/body/eval_jaxpr/ppermute | solution.py:19
  221.9 4.5 %collective-permute-done = bf16[32,4096]{1,0:T(8,128)(2,1)S(1)} collective-permute-done((bf16[32,4096]{1,0:T(8,128)(2,1)S(1)}, bf16[32,4096]{1,0:T(8,128)(2,1)S(1)}, u32[]{:S(2)}, u32[]{:S(2)}) %collective-permute-start) | collective-permute-done | bytes 262176 | tf_op jit(solution)/shard_map/while/body/eval_jaxpr/ppermute | solution.py:19
  226.5 1.0 dynamic-slice_select_fusion.2
  227.5 18.7 %conditional.5 = ((bf16[32,4096]{1,0:T(8,128)(2,1)S(1)}, bf16[128,512]{1,0:T(8,128)(2,1)}, bf16[128,512]{1,0:T(8,128)(2,1)}, bf16[128,4096]{1,0:T(8,128)(2,1)})) conditional(s32[]{:T(128)} %convert_element_type.108, (bf16[32,4096]{1,0:T(8,128)(2,1)S(1)}, bf16[128,512]{1,0:T(8,128)(2,1)}, bf16[128,512]{1,0:T(8,128)(2,1)}, ...), branch_computations={%region_6.6_spmd, %region_7.10_spmd} | conditional | flops 373972352 | bytes 19241090 | solution.py:121
  227.5 1.0 convert_bitcast_fusion.1
  229.9 3.1 %fusion.45 = f32[32,512]{1,0:T(8,128)S(1)} fusion(bf16[4096,512]{1,0:T(8,128)(2,1)} %get-tuple-element.308, bf16[32,4096]{1,0:T(8,128)(2,1)S(1)} %get-tuple-element.301, f32[4096]{0:T(1024)S(1)} %bitcast.83, f32[32]{0:T(128)S(1)} %add_rsqrt_fusion.1), kind=kOutput, calls=%fused_computation.67 | convolution fusion | flops 134742016 | bytes 4538496 | tf_op jit(solution)/shard_map/while/body/eval_jaxpr/cond/branch_1_fun/dot_general | solution.py:92
  233.2 1.4 dynamic_update_slice.16
  236.1 3.1 %convolution_convert_fusion.1 = bf16[32,512]{1,0:T(8,128)(2,1)S(1)} fusion(bf16[4096,512]{1,0:T(8,128)(2,1)} %get-tuple-element.304, bf16[32,4096]{1,0:T(8,128)(2,1)S(1)} %get-tuple-element.301, f32[4096]{0:T(1024)S(1)} %bitcast.84, f32[32]{0:T(128)S(1)} %add_rsqrt_fusion.1), kind=kOutput, calls=%fused_computation.49 | convolution fusion | flops 134758400 | bytes 4505728 | tf_op jit(solution)/shard_map/while/body/eval_jaxpr/cond/branch_1_fun/dot_general | solution.py:93
  239.2 1.4 dynamic_update_slice.15
  241.8 1.9 convolution_bitcast_fusion.1
  244.4 1.9 dynamic_update_slice.17
  246.2 5.4 %collective-permute-start = (bf16[32,4096]{1,0:T(8,128)(2,1)S(1)}, bf16[32,4096]{1,0:T(8,128)(2,1)S(1)}, u32[]{:S(2)}, u32[]{:S(2)}) collective-permute-start(bf16[32,4096]{1,0:T(8,128)(2,1)S(1)} %get-tuple-element.486), channel_id=1, source_target_pairs={{0,16},{1,17},{2,18},{3,19},{4,20},{5,21},{6,22},{7,23},{8,24},{9,... | collective-permute-start | bytes 786440 | tf_op jit(solution)/shard_map/while/body/eval_jaxpr/ppermute | solution.py:19
  251.6 3.9 %collective-permute-done = bf16[32,4096]{1,0:T(8,128)(2,1)S(1)} collective-permute-done((bf16[32,4096]{1,0:T(8,128)(2,1)S(1)}, bf16[32,4096]{1,0:T(8,128)(2,1)S(1)}, u32[]{:S(2)}, u32[]{:S(2)}) %collective-permute-start) | collective-permute-done | bytes 262176 | tf_op jit(solution)/shard_map/while/body/eval_jaxpr/ppermute | solution.py:19
  256.6 23.1 %collective-permute-start = (bf16[32,4096]{1,0:T(8,128)(2,1)S(1)}, bf16[32,4096]{1,0:T(8,128)(2,1)S(1)}, u32[]{:S(2)}, u32[]{:S(2)}) collective-permute-start(bf16[32,4096]{1,0:T(8,128)(2,1)S(1)} %get-tuple-element.486), channel_id=1, source_target_pairs={{0,16},{1,17},{2,18},{3,19},{4,20},{5,21},{6,22},{7,23},{8,24},{9,... | collective-permute-start | bytes 786440 | tf_op jit(solution)/shard_map/while/body/eval_jaxpr/ppermute | solution.py:19
  279.7 3.9 %collective-permute-done = bf16[32,4096]{1,0:T(8,128)(2,1)S(1)} collective-permute-done((bf16[32,4096]{1,0:T(8,128)(2,1)S(1)}, bf16[32,4096]{1,0:T(8,128)(2,1)S(1)}, u32[]{:S(2)}, u32[]{:S(2)}) %collective-permute-start) | collective-permute-done | bytes 262176 | tf_op jit(solution)/shard_map/while/body/eval_jaxpr/ppermute | solution.py:19
  (102 shorter events, 27.3 us)
Async XLA Ops:
  6.5 26.4 %all-gather.6.cloned.1.call-start = ((), (), s32[]{:S(2)}) async-start(), calls=%async_computation | async-start | bytes 1572864 | tf_op jit(solution)/shard_map/all_gather | solution.py:66
  7.3 78.2 %all-gather.8.cloned.1.call-start = ((), (), s32[]{:S(2)}) async-start(), calls=%async_computation.1 | async-start | bytes 4456448 | tf_op jit(solution)/shard_map/all_gather | solution.py:76
  8.0 128.6 %all-gather.10.cloned.1.call-start = ((), (), s32[]{:S(2)}) async-start(), calls=%async_computation.2 | async-start | bytes 4456448 | tf_op jit(solution)/shard_map/all_gather | solution.py:75
  136.6 2.4 copy-start
  158.7 7.5 %collective-permute-start.1 = (bf16[32,4096]{1,0:T(8,128)(2,1)S(1)}, bf16[32,4096]{1,0:T(8,128)(2,1)S(1)}, u32[]{:S(2)}, u32[]{:S(2)}) collective-permute-start(bf16[32,4096]{1,0:T(8,128)(2,1)S(1)} %get-tuple-element.334), channel_id=1, source_target_pairs={{0,16},{1,17},{2,18},{3,19},{4,20},{5,21},{6,22},{7,23},{8,24},{9,... | collective-permute-start | bytes 786440 | tf_op jit(solution)/shard_map/ppermute | solution.py:19
  167.3 2.4 copy-start.1
  187.0 9.8 %collective-permute-start = (bf16[32,4096]{1,0:T(8,128)(2,1)S(1)}, bf16[32,4096]{1,0:T(8,128)(2,1)S(1)}, u32[]{:S(2)}, u32[]{:S(2)}) collective-permute-start(bf16[32,4096]{1,0:T(8,128)(2,1)S(1)} %get-tuple-element.486), channel_id=1, source_target_pairs={{0,16},{1,17},{2,18},{3,19},{4,20},{5,21},{6,22},{7,23},{8,24},{9,... | collective-permute-start | bytes 786440 | tf_op jit(solution)/shard_map/while/body/eval_jaxpr/ppermute | solution.py:19
  197.8 2.4 copy-start.1
  217.6 8.9 %collective-permute-start = (bf16[32,4096]{1,0:T(8,128)(2,1)S(1)}, bf16[32,4096]{1,0:T(8,128)(2,1)S(1)}, u32[]{:S(2)}, u32[]{:S(2)}) collective-permute-start(bf16[32,4096]{1,0:T(8,128)(2,1)S(1)} %get-tuple-element.486), channel_id=1, source_target_pairs={{0,16},{1,17},{2,18},{3,19},{4,20},{5,21},{6,22},{7,23},{8,24},{9,... | collective-permute-start | bytes 786440 | tf_op jit(solution)/shard_map/while/body/eval_jaxpr/ppermute | solution.py:19
  227.5 2.4 copy-start.1
  246.2 9.3 %collective-permute-start = (bf16[32,4096]{1,0:T(8,128)(2,1)S(1)}, bf16[32,4096]{1,0:T(8,128)(2,1)S(1)}, u32[]{:S(2)}, u32[]{:S(2)}) collective-permute-start(bf16[32,4096]{1,0:T(8,128)(2,1)S(1)} %get-tuple-element.486), channel_id=1, source_target_pairs={{0,16},{1,17},{2,18},{3,19},{4,20},{5,21},{6,22},{7,23},{8,24},{9,... | collective-permute-start | bytes 786440 | tf_op jit(solution)/shard_map/while/body/eval_jaxpr/ppermute | solution.py:19
  256.6 27.0 %collective-permute-start = (bf16[32,4096]{1,0:T(8,128)(2,1)S(1)}, bf16[32,4096]{1,0:T(8,128)(2,1)S(1)}, u32[]{:S(2)}, u32[]{:S(2)}) collective-permute-start(bf16[32,4096]{1,0:T(8,128)(2,1)S(1)} %get-tuple-element.486), channel_id=1, source_target_pairs={{0,16},{1,17},{2,18},{3,19},{4,20},{5,21},{6,22},{7,23},{8,24},{9,... | collective-permute-start | bytes 786440 | tf_op jit(solution)/shard_map/while/body/eval_jaxpr/ppermute | solution.py:19
Sparse Core Ops, SparseCore 0:
  8.9 23.9 all-gather.5
  35.1 50.3 all-gather.7
  87.7 48.8 all-gather.9
where the time goes:
time: 292 us; the launch traced here: 290 us
  waiting for transfers between devices  153 us (52%)
  starting transfers between devices  38.7 us (13%)
  matrix products  35.4 us (12%)
  local copies, waits for them, and re-layouts  34.2 us (12%)
  other arithmetic  15.4 us (5%)
  between operations  13.1 us (4%)
    all_gather x1, waiting for transfers between devices, body(): lax.all_gather(value_weight[0], 'fsdp', axis=0, tiled=True)  51.6 us
    all_gather x1, waiting for transfers between devices, body(): lax.all_gather(key_weight[0], 'fsdp', axis=0, tiled=True)  51.1 us
    ppermute x5, starting transfers between devices, from_behind(): return lax.ppermute(value, axis, pairs)  38.6 us
    all_gather x1, waiting for transfers between devices, body(): whole_in = lax.all_gather(hidden_in, 'section', axis=1, tiled=True)[0]  24.2 us
    ppermute x5, waiting for transfers between devices, from_behind(): return lax.ppermute(value, axis, pairs)  23.8 us
    dot_general x4, matrix products, process(): key_new = jnp.dot(normed, key_full, preferred_element_type=jnp.float32)  12.2 us
    dot_general x4, matrix products, process(): value_new = jnp.dot(normed, value_full, preferred_element_type=jnp.float32)  12.2 us
    dynamic_update_slice x4, local copies, waits for them, and re-layouts, process(): outputs = lax.dynamic_update_slice_in_dim(outputs, result, row_start, 0)  10.2 us
  transfers between devices with their start and end apart: 8, of which 8 were waited for; matrix products, arithmetic and copies ran while one was open for 0% of the time, Pallas kernels for 0%

commit v1 on v0

v1 whole, which is shorter than its diff:
```python
import functools
import math

import jax
import jax.numpy as jnp
import numpy as np
from jax import lax
from jax.experimental import pallas as pl
from jax.experimental.pallas import tpu as pltpu
from jax.sharding import PartitionSpec as P

HD = 128
EPS = 1e-05
MESH = pl.DeviceIdType.MESH


def rope_tables(rows):
    half = HD // 2
    frequency = np.exp(np.arange(half, dtype=np.float32) * np.float32(-2.0 * math.log(10000.0) / HD))
    angles = np.arange(rows, dtype=np.float32)[:, None] * frequency[None, :].astype(np.float32)
    cosine, sine = np.cos(angles), np.sin(angles)
    return (
        np.concatenate([cosine, cosine], 1).astype(np.float32),
        np.concatenate([-sine, sine], 1).astype(np.float32),
    )


def rope(u, cosine, sine):
    return u * cosine + pltpu.roll(u, HD // 2, 1) * sine


def kernel(
    n, sections, outer, inner,
    hid, q_in, kw, vw, gain, cos_ref, sin_ref,
    out,
    w, xin, xs, qs, qp, normed, acc, kv, kvp,
    w_recv, w_send, own_sem, hid_recv, hid_send, hid_own, q_sem, kv_sem, x_sem,
):
    s = lax.axis_index("section")
    f = lax.axis_index("fsdp")
    core = lax.rem(f, 2)
    chip = f // 2
    i = lax.rem(chip, inner)
    o = chip // inner
    rows, width = xs.shape
    part = hid.shape[1]
    kvw = kw.shape[2]
    kv_heads = kvw // HD
    group = width // kvw
    depth = kw.shape[1]

    def index(oo, ii, cc):
        return (oo * inner + ii) * 2 + cc

    own_k = pltpu.make_async_copy(kw.at[0], w.at[f, 0], own_sem.at[0])
    own_v = pltpu.make_async_copy(vw.at[0], w.at[f, 1], own_sem.at[1])
    own_k.start()
    own_v.start()

    targets = (
        (o > 0, index(o - 1, i, core)),
        (o < outer - 1, index(o + 1, i, core)),
        (i > 0, index(o, i - 1, core)),
        (i < inner - 1, index(o, i + 1, core)),
        (None, index(o, i, 1 - core)),
    )

    barrier = pltpu.get_barrier_semaphore()
    for cond, target in targets:
        def greet(target=target):
            pl.semaphore_signal(barrier, inc=1, device_id={"fsdp": target}, device_id_type=MESH)
        if cond is None:
            greet()
        else:
            pl.when(cond)(greet)
    for step in range(1, sections):
        pl.semaphore_signal(
            barrier, inc=1, device_id={"section": lax.rem(s + step, sections)}, device_id_type=MESH
        )
    expected = (
        jnp.where(o > 0, 1, 0) + jnp.where(o < outer - 1, 1, 0)
        + jnp.where(i > 0, 1, 0) + jnp.where(i < inner - 1, 1, 0) + sections
    )
    pl.semaphore_wait(barrier, expected)

    def w_copy(way, origin):
        return pltpu.make_async_remote_copy(
            src_ref=w.at[origin], dst_ref=w.at[origin],
            send_sem=w_send.at[way, origin], recv_sem=w_recv.at[origin],
            device_id={"fsdp": targets[way][1]}, device_id_type=MESH,
        )

    def w_start(way, origin):
        cond = targets[way][0]
        if cond is None:
            w_copy(way, origin).start()
        else:
            pl.when(cond)(lambda: w_copy(way, origin).start())

    own_k.wait()
    own_v.wait()
    for way in range(5):
        w_start(way, f)

    mine = pl.ds(pl.multiple_of(s * part, part), part)

    def hid_copy(to):
        dst = xs if to == 0 else xin
        return pltpu.make_async_remote_copy(
            src_ref=hid.at[0], dst_ref=dst.at[mine], send_sem=hid_send.at[to],
            recv_sem=hid_recv.at[s], device_id={"section": to}, device_id_type=MESH,
        )

    def hid_local(to):
        dst = xs if to == 0 else xin
        return pltpu.make_async_copy(hid.at[0], dst.at[mine], hid_own)

    for to in range(min(2, sections)):
        pl.when(s != to)(lambda to=to: hid_copy(to).start())
        pl.when(s == to)(lambda to=to: hid_local(to).start())

    q_copy = pltpu.make_async_remote_copy(
        src_ref=q_in.at[0, 0], dst_ref=qp, send_sem=q_sem.at[0], recv_sem=q_sem.at[1],
        device_id={"section": jnp.minimum(s + 1, sections - 1)}, device_id_type=MESH,
    )
    kv_copy = pltpu.make_async_remote_copy(
        src_ref=kv, dst_ref=kvp, send_sem=kv_sem.at[0], recv_sem=kv_sem.at[1],
        device_id={"section": jnp.minimum(s + 1, sections - 1)}, device_id_type=MESH,
    )
    x_copy = pltpu.make_async_remote_copy(
        src_ref=xs, dst_ref=xin, send_sem=x_sem.at[0], recv_sem=x_sem.at[1],
        device_id={"section": jnp.minimum(s + 1, sections - 1)}, device_id_type=MESH,
    )
    last = s == sections - 1
    pl.when(jnp.logical_not(last))(lambda: q_copy.start())

    q_load = pltpu.make_async_copy(q_in.at[0, 0], qs, own_sem.at[0])
    q_load.start()
    q_load.wait()

    def rope_queries(ref):
        def one(h, _):
            cols = pl.ds(pl.multiple_of(h * HD, HD), HD)
            u = ref[:, cols].astype(jnp.float32)
            ref[:, cols] = rope(u, cos_ref[...], sin_ref[...]).astype(jnp.bfloat16)
            return 0
        lax.fori_loop(0, width // HD, one, 0)

    rope_queries(qs)

    def hid_arrive(to):
        hid_local(to).wait()
        dst = xs if to == 0 else xin
        for step in range(1, sections):
            j = lax.rem(to + step, sections)
            pltpu.make_async_remote_copy(
                src_ref=hid.at[0], dst_ref=dst.at[pl.ds(j * part, part)],
                send_sem=hid_send.at[to], recv_sem=hid_recv.at[j],
                device_id={"section": to}, device_id_type=MESH,
            ).wait_recv()

    block = 16

    def norm():
        def one(r, _):
            at = pl.ds(pl.multiple_of(r * block, block), block)
            x = xs[at, :].astype(jnp.float32)
            mean_square = jnp.mean(x * x, axis=-1, keepdims=True)
            y = (x * lax.rsqrt(mean_square + EPS) * gain[...]).astype(jnp.bfloat16)
            for pair in range(n // 2):
                normed[pair, at, :] = y[:, pair * 2 * depth:(pair + 1) * 2 * depth]
            return 0
        lax.fori_loop(0, rows // block, one, 0)

    def project(pair):
        a = normed[pair]
        for half in range(2):
            b = w[pl.ds(pair * 2, 2), half].reshape(2 * depth, kvw)
            acc[half] += jnp.dot(a, b, preferred_element_type=jnp.float32)

    acc[...] = jnp.zeros_like(acc)

    def arrive(origin, ways):
        w_copy(4, origin).wait_recv()
        for way in ways:
            w_start(way, origin)

    def spread(t, c, t_in, receive):
        for sign, way in ((-1, 1), (1, 0)):
            far = o - t if sign < 0 else o + t
            there = (far >= 0) if sign < 0 else (far < outer)
            pl.when(there)(lambda far=far, way=way: receive(index(far, i, c), (way, 2, 3, 4)))

    def spread_inner(t, c, receive):
        for sign in (-1, 1):
            far = o - t if sign < 0 else o + t
            there = (far >= 0) if sign < 0 else ((far < outer) & (t > 0))
            for d in range(1, inner):
                pl.when(there & (i - d >= 0))(
                    lambda far=far, d=d: receive(index(far, i - d, c), (3, 4)))
                pl.when(there & (i + d < inner))(
                    lambda far=far, d=d: receive(index(far, i + d, c), (2, 4)))

    def from_other(origin, ways):
        arrive(origin, ())

    def project_pair(origin, ways):
        project(origin // 2)

    def step(t, _):
        spread(t + 1, core, t, arrive)

        @pl.when((t == 0) & (s == 0))
        def _():
            hid_arrive(0)
            norm()

        @pl.when(t == 0)
        def _():
            from_other(index(o, i, 1 - core), ())

        spread_inner(t, core, arrive)
        spread(t + 1, 1 - core, t, from_other)
        spread_inner(t, 1 - core, from_other)

        @pl.when(s == 0)
        def _():
            pl.when(t == 0)(lambda: project(chip))
            spread(t + 1, core, t, project_pair)
            spread_inner(t, core, project_pair)

        return 0

    lax.fori_loop(0, outer, step, 0)

    row = lax.broadcasted_iota(jnp.int32, (rows, rows), 0)
    col = lax.broadcasted_iota(jnp.int32, (rows, rows), 1)
    scale = math.log2(math.e) / math.sqrt(HD)

    def attend(q_ref, kv_ref, x_ref, o_write):
        ones = jnp.ones((rows, HD), jnp.bfloat16)
        allowed = (col <= row)[None]

        def one(g, _):
            at = pl.ds(pl.multiple_of(g * HD, HD), HD)
            k = kv_ref[0, :, at]
            v = jnp.concatenate([kv_ref[1, :, at], ones], axis=1)
            base = g * group * HD
            cols = [pl.ds(pl.multiple_of(base + h * HD, HD), HD) for h in range(group)]
            q = jnp.concatenate([q_ref[:, c] for c in cols], axis=0)
            scores = lax.dot_general(q, k, (((1,), (1,)), ((), ())), preferred_element_type=jnp.float32)
            scores = jnp.where(allowed, scores.reshape(group, rows, rows), -1e30)
            top = jnp.max(scores, axis=-1, keepdims=True)
            p = jnp.exp2((scores - top) * scale).astype(jnp.bfloat16).reshape(group * rows, rows)
            mixed = jnp.dot(p, v, preferred_element_type=jnp.float32)
            mixed = mixed[:, :HD] / mixed[:, HD:]
            for h in range(group):
                o_write(cols[h], (
                    x_ref[:, cols[h]].astype(jnp.float32) + mixed[h * rows:(h + 1) * rows]
                ).astype(jnp.bfloat16))
            return 0

        lax.fori_loop(0, kv_heads, one, 0)

    def write_xs(c, value):
        xs[:, c] = value

    def write_out(c, value):
        out[0, 0, :, c] = value

    @pl.when(s > 0)
    def _():
        q_copy.wait_recv()
        rope_queries(qp)
        pl.when(s == 1)(lambda: hid_arrive(1))
        if sections > 2:
            pl.when(s > 1)(lambda: x_copy.wait_recv())
        kv_copy.wait_recv()
        attend(qp, kvp, xin, write_xs)
        if sections > 2:
            pl.when(jnp.logical_not(last))(lambda: x_copy.start())
        norm()
        def one(j, _):
            project(j)
            return 0
        lax.fori_loop(0, n // 2, one, 0)

    for h in range(kv_heads):
        at = slice(h * HD, (h + 1) * HD)
        kv[0, :, at] = rope(acc[0, :, at], cos_ref[...], sin_ref[...]).astype(jnp.bfloat16)
    kv[1] = acc[1].astype(jnp.bfloat16)
    pl.when(jnp.logical_not(last))(lambda: kv_copy.start())
    attend(qs, kv, xs, write_out)

    def drain(origin, ways):
        for way in ways:
            cond = targets[way][0]
            if cond is None:
                w_copy(way, origin).wait_send()
            else:
                pl.when(cond)(lambda way=way: w_copy(way, origin).wait_send())

    drain(f, range(5))

    def drain_step(t, _):
        spread(t + 1, core, t, drain)
        spread_inner(t, core, drain)
        return 0

    lax.fori_loop(0, outer, drain_step, 0)
    for to in range(min(2, sections)):
        pl.when(s != to)(lambda to=to: hid_copy(to).wait_send())

    @pl.when(jnp.logical_not(last))
    def _():
        q_copy.wait_send()
        kv_copy.wait_send()
        if sections > 2:
            pl.when(s > 0)(lambda: x_copy.wait_send())


def solution(mesh):
    sections, n = mesh.shape["section"], mesh.shape["fsdp"]
    chips = n // 2
    outer = 4 if chips % 4 == 0 else 1
    inner = chips // outer

    def body(hidden_in, queries, key_weight, value_weight, norm_gain):
        rows, width = queries.shape[2:]
        depth, kvw = key_weight.shape[1:]
        cosine, sine = rope_tables(rows)
        hbm = pl.BlockSpec(memory_space=pl.ANY)
        vmem = pl.BlockSpec(memory_space=pltpu.VMEM)
        dma = pltpu.SemaphoreType.DMA
        bf16, f32 = jnp.bfloat16, jnp.float32
        return pl.pallas_call(
            functools.partial(kernel, n, sections, outer, inner),
            out_shape=jax.ShapeDtypeStruct(queries.shape, bf16),
            in_specs=[hbm] * 4 + [vmem] * 3,
            out_specs=vmem,
            scratch_shapes=[
                pltpu.VMEM((n, 2, depth, kvw), bf16),
                pltpu.VMEM((rows, width), bf16),
                pltpu.VMEM((rows, width), bf16),
                pltpu.VMEM((rows, width), bf16),
                pltpu.VMEM((rows, width), bf16),
                pltpu.VMEM((n // 2, rows, 2 * depth), bf16),
                pltpu.VMEM((2, rows, kvw), f32),
                pltpu.VMEM((2, rows, kvw), bf16),
                pltpu.VMEM((2, rows, kvw), bf16),
                dma((n,)), dma((5, n)), dma((2,)), dma((sections,)), dma((2,)), dma,
                dma((2,)), dma((2,)), dma((2,)),
            ],
            compiler_params=pltpu.CompilerParams(
                collective_id=0, has_side_effects=True, vmem_limit_bytes=56 * 2**20
            ),
        )(hidden_in, queries, key_weight, value_weight, norm_gain, jnp.asarray(cosine), jnp.asarray(sine))

    placed = (
        P("fsdp", "section", None),
        P("section", "fsdp", None, None),
        P("section", "fsdp", None),
        P("section", "fsdp", None),
        P("section", None),
    )
    return jax.shard_map(
        body, mesh=mesh, in_specs=placed, out_specs=P("section", "fsdp", None, None), check_vma=False
    )
```

time: 292 us -> 73.3 us (0.25)
  the two profiles are of different devices: /device:TPU:0 before, /device:TPU:3 now
where the time goes in v1:
time: 73.3 us; the launch traced here: 73.1 us
  Pallas kernels  70.8 us (97%)
  local copies, waits for them, and re-layouts  2.29 us (3%)
    pallas_call x1, Pallas kernels, body(): pl.pallas_call(functools.partial(kernel, n, sections, outer, inner), out_...  70.8 us
    unnamed x1, local copies, waits for them, and re-layouts  2.29 us

profile of v1, /device:TPU:3, one launch (start us, length us, event | category | flops | bytes accessed | tf_op | source)
XLA Modules:
  0.0 73.1 jit_solution(581985598467754391)
XLA Ops:
  0.0 70.8 %shard_map.73 = bf16[1,1,128,4096]{3,2,1,0:T(8,128)(2,1)} custom-call(bf16[1,64,4096]{2,1,0:T(8,128)(2,1)} %hid.1, bf16[1,1,128,4096]{3,2,1,0:T(8,128)(2,1)} %q_in.1, bf16[1,256,512]{2,1,0:T(8,128)(2,1)} %kw.1, bf16[1,256,512]{2,1,0:T(8,128)(2,1)} %vw.1, f32[1,4096]{1,0:T(1,128)} %gain.1, f32[128,128]{1,0:T(8,128)} %constant.4.clone.cos_ref, ...), custom_call_target="tpu_custom_call" | custom-call | tf_op jit(solution)/shard_map/pallas_call | solution.py:336
  70.8 2.3 %copy.9 = bf16[1,1,128,4096]{3,2,1,0:T(8,128)(2,1)} copy(bf16[1,1,128,4096]{3,2,1,0:T(8,128)(2,1)} %shard_map.73) | data formatting | bytes 2097152

commit v2 on v1

--- a/solution.py
+++ b/solution.py
@@ -31,10 +31,10 @@
 
 def kernel(
     n, sections, outer, inner,
-    hid, q_in, kw, vw, gain, cos_ref, sin_ref,
+    hid, q_in, kw, vw, gain_in, cos_in, sin_in,
     out,
-    w, xin, xs, qs, qp, normed, acc, kv, kvp,
-    w_recv, w_send, own_sem, hid_recv, hid_send, hid_own, q_sem, kv_sem, x_sem,
+    w, xin, xs, qs, qp, normed, acc, kv, kvp, gain, cos_ref, sin_ref,
+    w_recv, w_send, own_sem, hid_recv, hid_send, hid_own, q_sem, kv_sem, x_sem, load_sem,
 ):
     s = lax.axis_index("section")
     f = lax.axis_index("fsdp")
@@ -56,6 +56,13 @@
     own_v = pltpu.make_async_copy(vw.at[0], w.at[f, 1], own_sem.at[1])
     own_k.start()
     own_v.start()
+    loads = [
+        pltpu.make_async_copy(src, dst, load_sem.at[at])
+        for at, (src, dst) in enumerate(
+            ((q_in.at[0, 0], qs), (gain_in, gain), (cos_in, cos_ref), (sin_in, sin_ref)))
+    ]
+    for load in loads:
+        load.start()
 
     targets = (
         (o > 0, index(o - 1, i, core)),
@@ -83,24 +90,32 @@
     )
     pl.semaphore_wait(barrier, expected)
 
-    def w_copy(way, origin):
+    few = max(16, depth // 8)
+    cuts = (pl.ds(0, depth - few), pl.ds(depth - few, few))
+
+    def w_copy(which, way, origin):
+        piece = w.at[origin, :, cuts[which]]
         return pltpu.make_async_remote_copy(
-            src_ref=w.at[origin], dst_ref=w.at[origin],
-            send_sem=w_send.at[way, origin], recv_sem=w_recv.at[origin],
+            src_ref=piece, dst_ref=piece,
+            send_sem=w_send.at[which, way, origin], recv_sem=w_recv.at[which, origin],
             device_id={"fsdp": targets[way][1]}, device_id_type=MESH,
         )
 
-    def w_start(way, origin):
+    def w_start(which, way, origin):
         cond = targets[way][0]
         if cond is None:
-            w_copy(way, origin).start()
+            w_copy(which, way, origin).start()
         else:
-            pl.when(cond)(lambda: w_copy(way, origin).start())
+            pl.when(cond)(lambda: w_copy(which, way, origin).start())
 
     own_k.wait()
     own_v.wait()
+    for way in (2, 3):
+        w_start(1, way, f)
     for way in range(5):
-        w_start(way, f)
+        w_start(0, way, f)
+    for way in (0, 1, 4):
+        w_start(1, way, f)
 
     mine = pl.ds(pl.multiple_of(s * part, part), part)
 
@@ -123,10 +138,12 @@
         src_ref=q_in.at[0, 0], dst_ref=qp, send_sem=q_sem.at[0], recv_sem=q_sem.at[1],
         device_id={"section": jnp.minimum(s + 1, sections - 1)}, device_id_type=MESH,
     )
-    kv_copy = pltpu.make_async_remote_copy(
-        src_ref=kv, dst_ref=kvp, send_sem=kv_sem.at[0], recv_sem=kv_sem.at[1],
-        device_id={"section": jnp.minimum(s + 1, sections - 1)}, device_id_type=MESH,
-    )
+    def kv_copy(g):
+        return pltpu.make_async_remote_copy(
+            src_ref=kv.at[g], dst_ref=kvp.at[g], send_sem=kv_sem.at[0, g], recv_sem=kv_sem.at[1, g],
+            device_id={"section": jnp.minimum(s + 1, sections - 1)}, device_id_type=MESH,
+        )
+
     x_copy = pltpu.make_async_remote_copy(
         src_ref=xs, dst_ref=xin, send_sem=x_sem.at[0], recv_sem=x_sem.at[1],
         device_id={"section": jnp.minimum(s + 1, sections - 1)}, device_id_type=MESH,
@@ -134,9 +151,8 @@
     last = s == sections - 1
     pl.when(jnp.logical_not(last))(lambda: q_copy.start())
 
-    q_load = pltpu.make_async_copy(q_in.at[0, 0], qs, own_sem.at[0])
-    q_load.start()
-    q_load.wait()
+    for load in loads:
+        load.wait()
 
     def rope_queries(ref):
         def one(h, _):
@@ -180,35 +196,51 @@
 
     acc[...] = jnp.zeros_like(acc)
 
-    def arrive(origin, ways):
-        w_copy(4, origin).wait_recv()
+    def arrive(which, origin, ways):
+        w_copy(which, 4, origin).wait_recv()
         for way in ways:
-            w_start(way, origin)
-
-    def spread(t, c, t_in, receive):
+            w_start(which, way, origin)
+
+    def relay(which, origin, ways):
+        arrive(which, origin, ways)
+
+    def from_other(which, origin, ways):
+        arrive(which, origin, ())
+
+    def project_pair(which, origin, ways):
+        if which == 0:
+            project(origin // 2)
+
+    def sides(t, act):
         for sign, way in ((-1, 1), (1, 0)):
             far = o - t if sign < 0 else o + t
-            there = (far >= 0) if sign < 0 else (far < outer)
-            pl.when(there)(lambda far=far, way=way: receive(index(far, i, c), (way, 2, 3, 4)))
-
-    def spread_inner(t, c, receive):
-        for sign in (-1, 1):
-            far = o - t if sign < 0 else o + t
             there = (far >= 0) if sign < 0 else ((far < outer) & (t > 0))
-            for d in range(1, inner):
-                pl.when(there & (i - d >= 0))(
-                    lambda far=far, d=d: receive(index(far, i - d, c), (3, 4)))
-                pl.when(there & (i + d < inner))(
-                    lambda far=far, d=d: receive(index(far, i + d, c), (2, 4)))
-
-    def from_other(origin, ways):
-        arrive(origin, ())
-
-    def project_pair(origin, ways):
-        project(origin // 2)
+            act(far, there, way)
+
+    def around(there, act):
+        for d in range(1, inner):
+            pl.when(there & (i - d >= 0))(lambda d=d: act(i - d, 3))
+            pl.when(there & (i + d < inner))(lambda d=d: act(i + d, 2))
+
+    def along_outer(t, c, receive):
+        def act(far, there, way):
+            pl.when(there)(lambda: receive(0, index(far, i, c), (way, 2, 3, 4)))
+            pl.when(there)(lambda: receive(1, index(far, i, c), (way, 4)))
+            around(there, lambda ii, _: receive(1, index(far, ii, c), (way, 4)))
+        sides(t, act)
+
+    def along_inner(t, c, receive):
+        def act(far, there, _):
+            around(there, lambda ii, way: receive(0, index(far, ii, c), (way, 4)))
+        sides(t, act)
+
+    def first_inner(c, receive):
+        around(o >= 0, lambda ii, way: receive(1, index(o, ii, c), (way, 0, 1, 4)))
+
+    first_inner(core, relay)
 
     def step(t, _):
-        spread(t + 1, core, t, arrive)
+        along_outer(t + 1, core, relay)
 
         @pl.when((t == 0) & (s == 0))
         def _():
@@ -217,17 +249,19 @@
 
         @pl.when(t == 0)
         def _():
-            from_other(index(o, i, 1 - core), ())
-
-        spread_inner(t, core, arrive)
-        spread(t + 1, 1 - core, t, from_other)
-        spread_inner(t, 1 - core, from_other)
+            for which in range(2):
+                arrive(which, index(o, i, 1 - core), ())
+            first_inner(1 - core, from_other)
+
+        along_inner(t, core, relay)
+        along_outer(t + 1, 1 - core, from_other)
+        along_inner(t, 1 - core, from_other)
 
         @pl.when(s == 0)
         def _():
             pl.when(t == 0)(lambda: project(chip))
-            spread(t + 1, core, t, project_pair)
-            spread_inner(t, core, project_pair)
+            along_outer(t + 1, core, project_pair)
+            along_inner(t, core, project_pair)
 
         return 0
 
@@ -237,14 +271,14 @@
     col = lax.broadcasted_iota(jnp.int32, (rows, rows), 1)
     scale = math.log2(math.e) / math.sqrt(HD)
 
-    def attend(q_ref, kv_ref, x_ref, o_write):
+    def attend(q_ref, kv_ref, x_ref, o_write, ready):
         ones = jnp.ones((rows, HD), jnp.bfloat16)
         allowed = (col <= row)[None]
 
         def one(g, _):
-            at = pl.ds(pl.multiple_of(g * HD, HD), HD)
-            k = kv_ref[0, :, at]
-            v = jnp.concatenate([kv_ref[1, :, at], ones], axis=1)
+            ready(g)
+            k = kv_ref[g, 0]
+            v = jnp.concatenate([kv_ref[g, 1], ones], axis=1)
             base = g * group * HD
             cols = [pl.ds(pl.multiple_of(base + h * HD, HD), HD) for h in range(group)]
             q = jnp.concatenate([q_ref[:, c] for c in cols], axis=0)
@@ -275,8 +309,7 @@
         pl.when(s == 1)(lambda: hid_arrive(1))
         if sections > 2:
             pl.when(s > 1)(lambda: x_copy.wait_recv())
-        kv_copy.wait_recv()
-        attend(qp, kvp, xin, write_xs)
+        attend(qp, kvp, xin, write_xs, lambda g: kv_copy(g).wait_recv())
         if sections > 2:
             pl.when(jnp.logical_not(last))(lambda: x_copy.start())
         norm()
@@ -287,24 +320,26 @@
 
     for h in range(kv_heads):
         at = slice(h * HD, (h + 1) * HD)
-        kv[0, :, at] = rope(acc[0, :, at], cos_ref[...], sin_ref[...]).astype(jnp.bfloat16)
-    kv[1] = acc[1].astype(jnp.bfloat16)
-    pl.when(jnp.logical_not(last))(lambda: kv_copy.start())
-    attend(qs, kv, xs, write_out)
-
-    def drain(origin, ways):
+        kv[h, 0] = rope(acc[0, :, at], cos_ref[...], sin_ref[...]).astype(jnp.bfloat16)
+        kv[h, 1] = acc[1, :, at].astype(jnp.bfloat16)
+        pl.when(jnp.logical_not(last))(lambda h=h: kv_copy(h).start())
+    attend(qs, kv, xs, write_out, lambda g: None)
+
+    def drain(which, origin, ways):
         for way in ways:
             cond = targets[way][0]
             if cond is None:
-                w_copy(way, origin).wait_send()
+                w_copy(which, way, origin).wait_send()
             else:
-                pl.when(cond)(lambda way=way: w_copy(way, origin).wait_send())
-
-    drain(f, range(5))
+                pl.when(cond)(lambda way=way: w_copy(which, way, origin).wait_send())
+
+    for which in range(2):
+        drain(which, f, range(5))
+    first_inner(core, drain)
 
     def drain_step(t, _):
-        spread(t + 1, core, t, drain)
-        spread_inner(t, core, drain)
+        along_outer(t + 1, core, drain)
+        along_inner(t, core, drain)
         return 0
 
     lax.fori_loop(0, outer, drain_step, 0)
@@ -314,7 +349,8 @@
     @pl.when(jnp.logical_not(last))
     def _():
         q_copy.wait_send()
-        kv_copy.wait_send()
+        for h in range(kv_heads):
+            kv_copy(h).wait_send()
         if sections > 2:
             pl.when(s > 0)(lambda: x_copy.wait_send())
 
@@ -329,14 +365,14 @@
         rows, width = queries.shape[2:]
         depth, kvw = key_weight.shape[1:]
         cosine, sine = rope_tables(rows)
-        hbm = pl.BlockSpec(memory_space=pl.ANY)
+        hbm = pl.BlockSpec(memory_space=pltpu.HBM)
         vmem = pl.BlockSpec(memory_space=pltpu.VMEM)
         dma = pltpu.SemaphoreType.DMA
         bf16, f32 = jnp.bfloat16, jnp.float32
         return pl.pallas_call(
             functools.partial(kernel, n, sections, outer, inner),
             out_shape=jax.ShapeDtypeStruct(queries.shape, bf16),
-            in_specs=[hbm] * 4 + [vmem] * 3,
+            in_specs=[hbm] * 7,
             out_specs=vmem,
             scratch_shapes=[
                 pltpu.VMEM((n, 2, depth, kvw), bf16),
@@ -346,13 +382,16 @@
                 pltpu.VMEM((rows, width), bf16),
                 pltpu.VMEM((n // 2, rows, 2 * depth), bf16),
                 pltpu.VMEM((2, rows, kvw), f32),
-                pltpu.VMEM((2, rows, kvw), bf16),
-                pltpu.VMEM((2, rows, kvw), bf16),
-                dma((n,)), dma((5, n)), dma((2,)), dma((sections,)), dma((2,)), dma,
-                dma((2,)), dma((2,)), dma((2,)),
+                pltpu.VMEM((kvw // HD, 2, rows, HD), bf16),
+                pltpu.VMEM((kvw // HD, 2, rows, HD), bf16),
+                pltpu.VMEM((1, width), f32),
+                pltpu.VMEM((rows, HD), f32),
+                pltpu.VMEM((rows, HD), f32),
+                dma((2, n)), dma((2, 5, n)), dma((2,)), dma((sections,)), dma((2,)), dma,
+                dma((2,)), dma((2, kvw // HD)), dma((2,)), dma((4,)),
             ],
             compiler_params=pltpu.CompilerParams(
-                collective_id=0, has_side_effects=True, vmem_limit_bytes=56 * 2**20
+                collective_id=0, has_side_effects=True, vmem_limit_bytes=28 * 2**20
             ),
         )(hidden_in, queries, key_weight, value_weight, norm_gain, jnp.asarray(cosine), jnp.asarray(sine))
 

time: 73.3 us -> 75.2 us (1.026)
  local copies, waits for them, and re-layouts: 2.29 us -> 7.53 us
  Pallas kernels: 70.8 us -> 67.3 us
    unnamed x1 -> x15, local copies, waits for them, and re-layouts: 2.29 us -> 7.53 us
    pallas_call x1, Pallas kernels: 70.8 us -> 67.3 us  [body(): pl.pallas_call(functools.partial(kernel, n, sections, outer, inner), out_...]
where the time goes in v2:
time: 75.2 us; the launch traced here: 74.8 us
  Pallas kernels  67.3 us (89%)
  local copies, waits for them, and re-layouts  7.53 us (10%)
    pallas_call x1, Pallas kernels, body(): pl.pallas_call(functools.partial(kernel, n, sections, outer, inner), out_...  67.3 us
    unnamed x15, local copies, waits for them, and re-layouts  7.53 us

profile of v2, /device:TPU:3, one launch (start us, length us, event | category | flops | bytes accessed | tf_op | source)
XLA Modules:
  0.0 74.8 jit_solution(7171764405719486401)
XLA Ops:
  0.0 0.0 copy-start
  0.0 1.2 %copy-done = bf16[1,1,128,4096]{3,2,1,0:T(8,128)(2,1)S(1)} copy-done((bf16[1,1,128,4096]{3,2,1,0:T(8,128)(2,1)S(1)}, bf16[1,1,128,4096]{3,2,1,0:T(8,128)(2,1)}, u32[]{:S(2)}) %copy-start) | copy-done | bytes 1048600
  1.2 0.0 copy-start.1
  1.2 1.0 %copy-done.1 = bf16[1,64,4096]{2,1,0:T(8,128)(2,1)S(1)} copy-done((bf16[1,64,4096]{2,1,0:T(8,128)(2,1)S(1)}, bf16[1,64,4096]{2,1,0:T(8,128)(2,1)}, u32[]{:S(2)}) %copy-start.1) | copy-done | bytes 524312
  2.3 0.0 copy-start.2
  2.3 0.9 %copy-done.2 = bf16[1,256,512]{2,1,0:T(8,128)(2,1)S(1)} copy-done((bf16[1,256,512]{2,1,0:T(8,128)(2,1)S(1)}, bf16[1,256,512]{2,1,0:T(8,128)(2,1)}, u32[]{:S(2)}) %copy-start.2) | copy-done | bytes 262168
  3.2 0.0 copy-start.3
  3.2 0.9 %copy-done.3 = bf16[1,256,512]{2,1,0:T(8,128)(2,1)S(1)} copy-done((bf16[1,256,512]{2,1,0:T(8,128)(2,1)S(1)}, bf16[1,256,512]{2,1,0:T(8,128)(2,1)}, u32[]{:S(2)}) %copy-start.3) | copy-done | bytes 262168
  4.2 0.0 copy-start.4
  4.2 0.8 %copy-done.4 = f32[128,128]{1,0:T(8,128)S(1)} copy-done((f32[128,128]{1,0:T(8,128)S(1)}, f32[128,128]{1,0:T(8,128)}, u32[]{:S(2)}) %copy-start.4) | copy-done | bytes 65560
  5.0 0.0 copy-start.5
  5.0 0.8 %copy-done.5 = f32[128,128]{1,0:T(8,128)S(1)} copy-done((f32[128,128]{1,0:T(8,128)S(1)}, f32[128,128]{1,0:T(8,128)}, u32[]{:S(2)}) %copy-start.5) | copy-done | bytes 65560
  5.8 0.0 copy-start.6
  5.9 0.7 copy-done.6
  6.6 67.3 %shard_map.73 = bf16[1,1,128,4096]{3,2,1,0:T(8,128)(2,1)S(1)} custom-call(bf16[1,64,4096]{2,1,0:T(8,128)(2,1)S(1)} %copy-done.1, bf16[1,1,128,4096]{3,2,1,0:T(8,128)(2,1)S(1)} %copy-done, bf16[1,256,512]{2,1,0:T(8,128)(2,1)S(1)} %copy-done.2, bf16[1,256,512]{2,1,0:T(8,128)(2,1)S(1)} %copy-done.3, f32[1,4096]{1,0:T(1,128)S(1)} %copy-done.6, ...), custom_call_target="tpu_custom_call" | custom-call | tf_op jit(solution)/shard_map/pallas_call | solution.py:372
  73.9 1.0 %copy.9 = bf16[1,1,128,4096]{3,2,1,0:T(8,128)(2,1)} copy(bf16[1,1,128,4096]{3,2,1,0:T(8,128)(2,1)S(1)} %shard_map.73) | data formatting | bytes 2097152
Async XLA Ops:
  0.0 1.2 %copy-start = (bf16[1,1,128,4096]{3,2,1,0:T(8,128)(2,1)S(1)}, bf16[1,1,128,4096]{3,2,1,0:T(8,128)(2,1)}, u32[]{:S(2)}) copy-start(bf16[1,1,128,4096]{3,2,1,0:T(8,128)(2,1)} %q_in.1) | copy-start | bytes 3145732
  1.2 1.0 %copy-start.1 = (bf16[1,64,4096]{2,1,0:T(8,128)(2,1)S(1)}, bf16[1,64,4096]{2,1,0:T(8,128)(2,1)}, u32[]{:S(2)}) copy-start(bf16[1,64,4096]{2,1,0:T(8,128)(2,1)} %hid.1) | copy-start | bytes 1572868
  2.3 0.9 %copy-start.2 = (bf16[1,256,512]{2,1,0:T(8,128)(2,1)S(1)}, bf16[1,256,512]{2,1,0:T(8,128)(2,1)}, u32[]{:S(2)}) copy-start(bf16[1,256,512]{2,1,0:T(8,128)(2,1)} %kw.1) | copy-start | bytes 786436
  3.2 0.9 %copy-start.3 = (bf16[1,256,512]{2,1,0:T(8,128)(2,1)S(1)}, bf16[1,256,512]{2,1,0:T(8,128)(2,1)}, u32[]{:S(2)}) copy-start(bf16[1,256,512]{2,1,0:T(8,128)(2,1)} %vw.1) | copy-start | bytes 786436
  4.2 0.8 %copy-start.4 = (f32[128,128]{1,0:T(8,128)S(1)}, f32[128,128]{1,0:T(8,128)}, u32[]{:S(2)}) copy-start(f32[128,128]{1,0:T(8,128)} %constant.5.clone.sin_in) | copy-start | bytes 196612
  5.0 0.8 %copy-start.5 = (f32[128,128]{1,0:T(8,128)S(1)}, f32[128,128]{1,0:T(8,128)}, u32[]{:S(2)}) copy-start(f32[128,128]{1,0:T(8,128)} %constant.4.clone.cos_in) | copy-start | bytes 196612
  5.8 0.7 copy-start.6

commit v3 on v2

--- a/solution.py
+++ b/solution.py
@@ -91,7 +91,9 @@
     pl.semaphore_wait(barrier, expected)
 
     few = max(16, depth // 8)
-    cuts = (pl.ds(0, depth - few), pl.ds(depth - few, few))
+    first = (depth - few + 16) // 32 * 16
+    cuts = (pl.ds(0, first), pl.ds(first, depth - few - first), pl.ds(depth - few, few))
+    mains, tail = (0, 1), 2
 
     def w_copy(which, way, origin):
         piece = w.at[origin, :, cuts[which]]
@@ -111,11 +113,12 @@
     own_k.wait()
     own_v.wait()
     for way in (2, 3):
-        w_start(1, way, f)
-    for way in range(5):
-        w_start(0, way, f)
+        w_start(tail, way, f)
+    for which in mains:
+        for way in range(5):
+            w_start(which, way, f)
     for way in (0, 1, 4):
-        w_start(1, way, f)
+        w_start(tail, way, f)
 
     mine = pl.ds(pl.multiple_of(s * part, part), part)
 
@@ -208,7 +211,7 @@
         arrive(which, origin, ())
 
     def project_pair(which, origin, ways):
-        if which == 0:
+        if which == tail - 1:
             project(origin // 2)
 
     def sides(t, act):
@@ -223,19 +226,24 @@
             pl.when(there & (i + d < inner))(lambda d=d: act(i + d, 2))
 
     def along_outer(t, c, receive):
-        def act(far, there, way):
-            pl.when(there)(lambda: receive(0, index(far, i, c), (way, 2, 3, 4)))
-            pl.when(there)(lambda: receive(1, index(far, i, c), (way, 4)))
-            around(there, lambda ii, _: receive(1, index(far, ii, c), (way, 4)))
-        sides(t, act)
+        for which in mains:
+            def act(far, there, way, which=which):
+                pl.when(there)(lambda: receive(which, index(far, i, c), (way, 2, 3, 4)))
+            sides(t, act)
+
+        def act_tail(far, there, way):
+            pl.when(there)(lambda: receive(tail, index(far, i, c), (way, 4)))
+            around(there, lambda ii, _: receive(tail, index(far, ii, c), (way, 4)))
+        sides(t, act_tail)
 
     def along_inner(t, c, receive):
-        def act(far, there, _):
-            around(there, lambda ii, way: receive(0, index(far, ii, c), (way, 4)))
-        sides(t, act)
+        for which in mains:
+            def act(far, there, _, which=which):
+                around(there, lambda ii, way: receive(which, index(far, ii, c), (way, 4)))
+            sides(t, act)
 
     def first_inner(c, receive):
-        around(o >= 0, lambda ii, way: receive(1, index(o, ii, c), (way, 0, 1, 4)))
+        around(o >= 0, lambda ii, way: receive(tail, index(o, ii, c), (way, 0, 1, 4)))
 
     first_inner(core, relay)
 
@@ -249,7 +257,7 @@
 
         @pl.when(t == 0)
         def _():
-            for which in range(2):
+            for which in (*mains, tail):
                 arrive(which, index(o, i, 1 - core), ())
             first_inner(1 - core, from_other)
 
@@ -333,7 +341,7 @@
             else:
                 pl.when(cond)(lambda way=way: w_copy(which, way, origin).wait_send())
 
-    for which in range(2):
+    for which in (*mains, tail):
         drain(which, f, range(5))
     first_inner(core, drain)
 
@@ -387,13 +395,16 @@
                 pltpu.VMEM((1, width), f32),
                 pltpu.VMEM((rows, HD), f32),
                 pltpu.VMEM((rows, HD), f32),
-                dma((2, n)), dma((2, 5, n)), dma((2,)), dma((sections,)), dma((2,)), dma,
+                dma((3, n)), dma((3, 5, n)), dma((2,)), dma((sections,)), dma((2,)), dma,
                 dma((2,)), dma((2, kvw // HD)), dma((2,)), dma((4,)),
             ],
             compiler_params=pltpu.CompilerParams(
                 collective_id=0, has_side_effects=True, vmem_limit_bytes=28 * 2**20
             ),
-        )(hidden_in, queries, key_weight, value_weight, norm_gain, jnp.asarray(cosine), jnp.asarray(sine))
+        )(*(
+            pltpu.with_memory_space_constraint(x, pltpu.HBM)
+            for x in (hidden_in, queries, key_weight, value_weight, norm_gain, jnp.asarray(cosine), jnp.asarray(sine))
+        ))
 
     placed = (
         P("fsdp", "section", None),

time: 75.2 us -> 65.1 us (0.87)
  local copies, waits for them, and re-layouts: 7.53 us -> 0.97 us
  Pallas kernels: 67.3 us -> 64 us
    unnamed x15 -> x1, local copies, waits for them, and re-layouts: 7.53 us -> 0.97 us
    pallas_call x1, Pallas kernels: 67.3 us -> 64 us  [body(): pl.pallas_call(functools.partial(kernel, n, sections, outer, inner), out_...]
where the time goes in v3:
time: 65.1 us; the launch traced here: 65 us
  Pallas kernels  64 us (98%)
  local copies, waits for them, and re-layouts  0.97 us (1%)
    pallas_call x1, Pallas kernels, body(): pl.pallas_call(functools.partial(kernel, n, sections, outer, inner), out_...  64 us

profile of v3, /device:TPU:3, one launch (start us, length us, event | category | flops | bytes accessed | tf_op | source)
XLA Modules:
  0.0 65.0 jit_solution(1056515498181626641)
XLA Ops:
  0.0 64.0 %shard_map.73 = bf16[1,1,128,4096]{3,2,1,0:T(8,128)(2,1)S(1)} custom-call(bf16[1,64,4096]{2,1,0:T(8,128)(2,1)} %hid.1, bf16[1,1,128,4096]{3,2,1,0:T(8,128)(2,1)} %q_in.1, bf16[1,256,512]{2,1,0:T(8,128)(2,1)} %kw.1, bf16[1,256,512]{2,1,0:T(8,128)(2,1)} %vw.1, f32[1,4096]{1,0:T(1,128)} %gain_in.1, f32[128,128]{1,0:T(8,128)} %constant.4.clone.cos_in, ...), custom_call_target="tpu_custom_call" | custom-call | tf_op jit(solution)/shard_map/pallas_call | solution.py:380
  64.0 1.0 %copy.9 = bf16[1,1,128,4096]{3,2,1,0:T(8,128)(2,1)} copy(bf16[1,1,128,4096]{3,2,1,0:T(8,128)(2,1)S(1)} %shard_map.73) | data formatting | bytes 2097152

commit v4 on v3

--- a/solution.py
+++ b/solution.py
@@ -91,9 +91,10 @@
     pl.semaphore_wait(barrier, expected)
 
     few = max(16, depth // 8)
-    first = (depth - few + 16) // 32 * 16
-    cuts = (pl.ds(0, first), pl.ds(first, depth - few - first), pl.ds(depth - few, few))
-    mains, tail = (0, 1), 2
+    third = (depth - few + 32) // 48 * 16
+    edges = (0, third, 2 * third, depth - few, depth)
+    cuts = tuple(pl.ds(a, b - a) for a, b in zip(edges[:-1], edges[1:]))
+    mains, tail = (0, 1, 2), 3
 
     def w_copy(which, way, origin):
         piece = w.at[origin, :, cuts[which]]
@@ -395,7 +396,7 @@
                 pltpu.VMEM((1, width), f32),
                 pltpu.VMEM((rows, HD), f32),
                 pltpu.VMEM((rows, HD), f32),
-                dma((3, n)), dma((3, 5, n)), dma((2,)), dma((sections,)), dma((2,)), dma,
+                dma((4, n)), dma((4, 5, n)), dma((2,)), dma((sections,)), dma((2,)), dma,
                 dma((2,)), dma((2, kvw // HD)), dma((2,)), dma((4,)),
             ],
             compiler_params=pltpu.CompilerParams(

time: 65.1 us -> 66 us (1.014)
  Pallas kernels: 64 us -> 64.9 us
    pallas_call x1, Pallas kernels: 64 us -> 64.9 us  [body(): pl.pallas_call(functools.partial(kernel, n, sections, outer, inner), out_...]
where the time goes in v4:
time: 66 us; the launch traced here: 65.8 us
  Pallas kernels  64.9 us (98%)
  local copies, waits for them, and re-layouts  0.97 us (1%)
    pallas_call x1, Pallas kernels, body(): pl.pallas_call(functools.partial(kernel, n, sections, outer, inner), out_...  64.9 us

profile of v4, /device:TPU:3, one launch (start us, length us, event | category | flops | bytes accessed | tf_op | source)
XLA Modules:
  0.0 65.8 jit_solution(8322197810212643582)
XLA Ops:
  0.0 64.9 %shard_map.73 = bf16[1,1,128,4096]{3,2,1,0:T(8,128)(2,1)S(1)} custom-call(bf16[1,64,4096]{2,1,0:T(8,128)(2,1)} %hid.1, bf16[1,1,128,4096]{3,2,1,0:T(8,128)(2,1)} %q_in.1, bf16[1,256,512]{2,1,0:T(8,128)(2,1)} %kw.1, bf16[1,256,512]{2,1,0:T(8,128)(2,1)} %vw.1, f32[1,4096]{1,0:T(1,128)} %gain_in.1, f32[128,128]{1,0:T(8,128)} %constant.4.clone.cos_in, ...), custom_call_target="tpu_custom_call" | custom-call | tf_op jit(solution)/shard_map/pallas_call | solution.py:381
  64.9 1.0 %copy.9 = bf16[1,1,128,4096]{3,2,1,0:T(8,128)(2,1)} copy(bf16[1,1,128,4096]{3,2,1,0:T(8,128)(2,1)S(1)} %shard_map.73) | data formatting | bytes 2097152
